TPU v7x, 1024 devices: a whole 4x8x16 slice. The times are simulated.
1024 devices in a mesh: gz: 16 (over y, core), xy: 64 (over z, x).
Axes of the slice: x: 4, y: 8, z: 16, core: 2. Of those that a mesh axis runs over, the one named last changes fastest.
Arguments:
- density: float32 [128, 8192, 128], P('gz', 'xy'), may hold values from -96 to 96
- live_slices: int32 [16, 64], replicated, may hold values from 1 to 8, as said below
- shear_slopes: float32 [2], replicated, may hold values from -0.12 to 0.12
- palette: float32 [3], replicated, may hold values from 0.5 to 2
- depth_order: int32 [2, 16], replicated, may hold values from 0 to 15, each once within a row
- tile_owner: int32 [2, 16], replicated, may hold values from 0 to 15, each once within a row
Outputs:
- owned_tiles: float32 [2, 4, 16, 512, 128], P(None, None, 'gz', 'xy')
Inputs may be any that keep to these rules, and one draw needn't show every extreme that they name: `live_slices`: some brick has all 8 slices live. `depth_order`: each row lists every slab once. `tile_owner`: each row names every index of gz once.
All inputs are finite; a program needn't handle non-finite values.
Results may differ from a plain program's by a relative error of at most 0.00042.
Values may be sent and summed in bfloat16 or wider, within the bound.
A program may use at most 32 MiB of HBM per device.

v0:
```python
import functools

import jax
import jax.numpy as jnp
from jax import lax
from jax.experimental import pallas as pl
from jax.experimental.pallas import tpu as pltpu
from jax.sharding import PartitionSpec as P

LIGHT = (0.48, 0.6, 0.64)
LOG2E = 1.4426950408889634
CHUNKS = ((0, 32), (32, 64), (64, 96), (96, 128))
F32, BF16 = jnp.float32, jnp.bfloat16


def spread(first, second, inside):
    return jnp.where(inside, jnp.where((first - second <= 4) & (second - first <= 4), 1.0, 0.0), 0.0)


def kernel(
    G, R, depth_axis, row_axis,
    live_ref, slopes_ref, palette_ref, order_ref, owner_ref, dens_ref,
    out_ref,
    ext, summed, rowed, smooth, dcol, band, layers, shear, sheared, outbox, inbox, inverse,
    local_sem, zsend, zrecv, rsend, rrecv, tsend, trecv,
):
    me = lax.axis_index(depth_axis)
    col = lax.axis_index(row_axis)
    CZ, CY, W = dens_ref.shape
    TR = CY // G
    NC = len(CHUNKS)
    has = {-1: me > 0, 1: me < G - 1}
    hasr = {-1: col > 0, 1: col < R - 1}
    at = lambda g, r: {depth_axis: g, row_axis: r}

    barrier = pltpu.get_barrier_semaphore()

    def greet(k, carry):
        pl.semaphore_signal(barrier, inc=1, device_id=at(lax.rem(me + k, G), col))
        return carry

    lax.fori_loop(1, G, greet, 0)
    for dr in (-1, 1):
        for dz in (-1, 0, 1):
            ok = hasr[dr] if dz == 0 else hasr[dr] & has[dz]

            @pl.when(ok)
            def _():
                pl.semaphore_signal(barrier, inc=1, device_id=at(me + dz, col + dr))

    local = pltpu.make_async_copy(dens_ref, ext.at[5:13, 8:136, :], local_sem)
    local.start()
    beside = hasr[-1].astype(jnp.int32) + hasr[1].astype(jnp.int32)
    above = has[-1].astype(jnp.int32) + has[1].astype(jnp.int32)
    pl.semaphore_wait(barrier, (G - 1) + beside * (1 + above))

    def zcopy(dz, k):
        lo, hi = CHUNKS[k]
        src = dens_ref.at[3:8, lo:hi, :] if dz == 1 else dens_ref.at[0:5, lo:hi, :]
        dst = ext.at[0:5, 8 + lo : 8 + hi, :] if dz == 1 else ext.at[13:18, 8 + lo : 8 + hi, :]
        side = (dz + 1) // 2
        return pltpu.make_async_remote_copy(
            src, dst, zsend.at[side, k], zrecv.at[side, k], device_id=at(me + dz, col)
        )

    def rcopy(dz, dr):
        zs, zd = {0: (slice(0, 8), slice(5, 13)), 1: (slice(3, 8), slice(0, 5)), -1: (slice(0, 5), slice(13, 18))}[dz]
        rs, rd = {1: (slice(120, 128), slice(0, 8)), -1: (slice(0, 8), slice(136, 144))}[dr]
        side = (dr + 1) // 2
        return pltpu.make_async_remote_copy(
            dens_ref.at[zs, rs, :], ext.at[zd, rd, :], rsend.at[side, dz + 1], rrecv.at[side, dz + 1],
            device_id=at(me + dz, col + dr),
        )

    zcopies = [(dz, k) for k in range(NC) for dz in (1, -1)]
    rcopies = [(dz, dr) for dr in (-1, 1) for dz in (1, -1, 0)]

    def allowed(dz, dr):
        return hasr[dr] if dz == 0 else hasr[dr] & has[dz]

    for dz in (1, -1):
        @pl.when(has[dz])
        def _():
            zcopy(dz, 0).start()
    for dz, dr in rcopies:
        @pl.when(allowed(dz, dr))
        def _():
            rcopy(dz, dr).start()
    for dz in (1, -1):
        @pl.when(has[dz])
        def _():
            for k in range(1, NC):
                zcopy(dz, k).start()

    for dz in (1, -1):
        @pl.when(jnp.logical_not(has[-dz]))
        def _():
            zd = slice(0, 5) if dz == 1 else slice(13, 18)
            ext[zd, :, :] = jnp.zeros((5, CY + 16, W), F32)
    for dr in (1, -1):
        @pl.when(jnp.logical_not(hasr[-dr]))
        def _():
            rd = slice(0, 8) if dr == 1 else slice(136, 144)
            ext[:, rd, :] = jnp.zeros((CZ + 10, 8, W), F32)

    def invert(d, carry):
        for v in range(2):
            found = jnp.int32(0)
            for t in range(G):
                found = jnp.maximum(found, t * (owner_ref[v, t] == d).astype(jnp.int32))
            inverse[v, d] = found
        return carry

    lax.fori_loop(0, G, invert, 0)

    source = lax.broadcasted_iota(jnp.int32, (W, W), 0)
    target = lax.broadcasted_iota(jnp.int32, (W, W), 1)
    ones = spread(source, target, True)
    diff = spread(source, target + 1, target + 1 < W) - spread(source, target - 1, target >= 1)
    for half in range(2):
        band[half * W : half * W + W, 0:W] = ones.astype(BF16)
        band[half * W : half * W + W, W : 2 * W] = diff.astype(BF16)

    offset = (source - target).astype(F32)

    def shears(z, carry):
        depth = (me * CZ + z).astype(F32) + (0.5 - 0.5 * CZ * G)
        for v in range(2):
            m = jnp.maximum(0.0, 1.0 - jnp.abs(offset + slopes_ref[v] * depth))
            shear[z, :, v * W : v * W + W] = m.astype(BF16)
        return carry

    lax.fori_loop(0, CZ, shears, 0)

    live = live_ref[me, col]
    brightest = jnp.maximum(jnp.maximum(palette_ref[0], palette_ref[1]), palette_ref[2])

    def depth_sums(lo, hi):
        def block(b, carry):
            rows = pl.ds(pl.multiple_of(lo + 8 * b, 8), 8)
            x = [ext[z, rows, :] for z in range(CZ + 10)]
            two = [x[i] + x[i + 1] for i in range(CZ + 8)]
            four = [two[i] + two[i + 2] for i in range(CZ + 6)]
            eight = [four[i] + four[i + 4] for i in range(CZ + 2)]
            for z in range(CZ + 2):
                summed[z, rows, :] = eight[z] + x[z + 8]
            return carry

        lax.fori_loop(0, (hi - lo) // 8, block, 0)

    def smooth_rows(lo, hi):
        def layer(z, carry):
            for j in range(lo, hi, 8):
                s = [summed[z, j + k : j + 8 + k, :] for k in range(9)]
                rowed[z, j : j + 8, :] = (
                    ((s[0] + s[1]) + (s[2] + s[3])) + ((s[4] + s[5]) + (s[6] + s[7])) + s[8]
                )
            return carry

        lax.fori_loop(0, CZ + 2, layer, 0)

    def smooth_cols(lo, hi):
        def layer(z, carry):
            x = rowed[z, lo:hi, :]
            high = x.astype(BF16)
            low = (x - high.astype(F32)).astype(BF16)
            both = jnp.dot(
                jnp.concatenate([high, low], axis=1), band[...], preferred_element_type=F32
            )
            smooth[z, lo:hi, :] = both[:, 0:W]
            dcol[z, lo:hi, :] = both[:, W : 2 * W]
            return carry

        lax.fori_loop(0, CZ + 2, layer, 0)

    def shade(lo, hi):
        def layer(z, carry):
            alive = (z < live).astype(jnp.int32).astype(F32)
            bright_of = alive * brightest
            for r in range(lo, hi, 16):
                q = r + 4
                n = 16
                center = smooth[z + 1, q : q + n, :]
                dz = smooth[z + 2, q : q + n, :] - smooth[z, q : q + n, :]
                dr = smooth[z + 1, q + 1 : q + n + 1, :] - smooth[z + 1, q - 1 : q + n - 1, :]
                dc = dcol[z + 1, q : q + n, :]
                along = jnp.maximum(0.0, LIGHT[0] * dz + LIGHT[1] * dr + LIGHT[2] * dc)
                facing = along * lax.rsqrt(dz * dz + dr * dr + dc * dc + 0.01 * 1458.0 * 1458.0)
                y = center * (2.0 / 729.0)
                soft = jnp.maximum(y, 0.0) + jnp.log(1.0 + jnp.exp(-jnp.abs(y)))
                opacity = 1.0 - jnp.exp(soft * (-3.0 / (CZ * G)))
                layers[z, 0, r : r + n, :] = (opacity * (0.25 + 0.75 * facing) * bright_of).astype(BF16)
                layers[z, 1, r : r + n, :] = (opacity * alive).astype(BF16)
            return carry

        lax.fori_loop(0, CZ, layer, 0)

    def shear_rows(lo, hi):
        def layer(z, carry):
            lhs = layers[z, :, lo:hi, :].reshape(2 * (hi - lo), W)
            out = jnp.dot(lhs, shear[z], preferred_element_type=F32)
            sheared[z, :, lo // TR : hi // TR] = out.reshape(2, (hi - lo) // TR, TR, 2 * W)
            return carry

        lax.fori_loop(0, CZ, layer, 0)

    def clear(lo, hi):
        for dz in (-1, 1):
            @pl.when(jnp.logical_not(has[dz]))
            def _():
                smooth[0 if dz == -1 else CZ + 1, lo:hi, :] = jnp.zeros((hi - lo, W), F32)

    local.wait()
    for dz, dr in rcopies:
        @pl.when(allowed(-dz, -dr))
        def _():
            rcopy(dz, dr).wait_recv()

    depth_sums(0, 8)
    depth_sums(CY + 8, CY + 16)
    done_rows, done_smooth = 0, 0
    for k in range(NC):
        for dz in (1, -1):
            @pl.when(has[-dz])
            def _():
                zcopy(dz, k).wait_recv()
        lo, hi = CHUNKS[k]
        depth_sums(8 + lo, 8 + hi)
        last = k == NC - 1
        upto = CY + 8 if last else hi
        smooth_rows(done_smooth, upto)
        smooth_cols(done_smooth, upto)
        clear(done_smooth, upto)
        if k == 0:
            @pl.when(jnp.logical_not(hasr[-1]))
            def _():
                smooth[:, 0:4, :] = jnp.zeros((CZ + 2, 4, W), F32)
        if last:
            @pl.when(jnp.logical_not(hasr[1]))
            def _():
                smooth[:, CY + 4 : CY + 8, :] = jnp.zeros((CZ + 2, 4, W), F32)
        done_smooth = upto
        shaded = CY if last else hi - 16
        shade(done_rows, shaded)
        shear_rows(done_rows, shaded)
        done_rows = shaded

    def tcopy(d):
        return pltpu.make_async_remote_copy(
            outbox.at[d], inbox.at[me], tsend.at[d], trecv.at[me], device_id=at(d, col)
        )

    def march(d, box, slot):
        for v in range(2):
            tile = inverse[v, d]
            shaded, transmit = None, None
            for z in range(CZ) if v == 0 else range(CZ - 1, -1, -1):
                b = sheared[z, 0, tile, :, v * W : v * W + W]
                a = sheared[z, 1, tile, :, v * W : v * W + W]
                shaded = b if shaded is None else shaded + transmit * b
                transmit = 1.0 - a if transmit is None else transmit * (1.0 - a)
            box[slot, v, 0] = shaded
            box[slot, v, 1] = transmit

    def send(k, carry):
        d = lax.rem(me + k, G)
        march(d, outbox, d)
        tcopy(d).start()
        return carry

    lax.fori_loop(1, G, send, 0)
    march(me, inbox, me)

    def receive(k, carry):
        s = lax.rem(me + G - k, G)
        pltpu.make_async_remote_copy(
            outbox.at[s], inbox.at[s], tsend.at[s], trecv.at[s], device_id=at(s, col)
        ).wait_recv()
        return carry

    lax.fori_loop(1, G, receive, 0)

    for v in range(2):
        def blend(i, carry):
            shaded, transmit = carry
            s = order_ref[v, i]
            return shaded + transmit * inbox[s, v, 0], transmit * inbox[s, v, 1]

        shaded, transmit = lax.fori_loop(
            0, G, blend, (jnp.zeros((TR, W), F32), jnp.ones((TR, W), F32)), unroll=True
        )
        for c in range(3):
            out_ref[v, c] = shaded * (palette_ref[c] / brightest)
        out_ref[v, 3] = 1.0 - transmit

    for dz in (1, -1):
        @pl.when(has[dz])
        def _():
            for k in range(NC):
                zcopy(dz, k).wait_send()
    for dz, dr in rcopies:
        @pl.when(allowed(dz, dr))
        def _():
            rcopy(dz, dr).wait_send()

    def sent(k, carry):
        d = lax.rem(me + k, G)
        tcopy(d).wait_send()
        return carry

    lax.fori_loop(1, G, sent, 0)


def solution(mesh):
    depth_axis, row_axis = mesh.axis_names
    G, R = mesh.shape[depth_axis], mesh.shape[row_axis]

    def body(density, live_slices, shear_slopes, palette, depth_order, tile_owner):
        CZ, CY, W = density.shape
        TR = CY // G
        smem = pl.BlockSpec(memory_space=pltpu.SMEM)
        dma = pltpu.SemaphoreType.DMA
        NC = len(CHUNKS)
        out = pl.pallas_call(
            functools.partial(kernel, G, R, depth_axis, row_axis),
            out_shape=jax.ShapeDtypeStruct((2, 4, TR, W), F32),
            in_specs=[smem] * 5 + [pl.BlockSpec(memory_space=pl.ANY)],
            out_specs=pl.BlockSpec(memory_space=pltpu.VMEM),
            scratch_shapes=[
                pltpu.VMEM((CZ + 10, CY + 16, W), F32),
                pltpu.VMEM((CZ + 2, CY + 16, W), F32),
                pltpu.VMEM((CZ + 2, CY + 8, W), F32),
                pltpu.VMEM((CZ + 2, CY + 8, W), F32),
                pltpu.VMEM((CZ + 2, CY + 8, W), F32),
                pltpu.VMEM((2 * W, 2 * W), BF16),
                pltpu.VMEM((CZ, 2, CY, W), BF16),
                pltpu.VMEM((CZ, W, 2 * W), BF16),
                pltpu.VMEM((CZ, 2, G, TR, 2 * W), F32),
                pltpu.VMEM((G, 2, 2, TR, W), F32),
                pltpu.VMEM((G, 2, 2, TR, W), F32),
                pltpu.SMEM((2, G), jnp.int32),
                dma,
                dma((2, NC)),
                dma((2, NC)),
                dma((2, 3)),
                dma((2, 3)),
                dma((G,)),
                dma((G,)),
            ],
            compiler_params=pltpu.CompilerParams(collective_id=0, has_side_effects=True),
        )(live_slices, shear_slopes, palette, depth_order, tile_owner, density)
        return out[:, :, None]

    placed = (P(depth_axis, row_axis, None), P(), P(), P(), P(), P())
    return jax.shard_map(
        body,
        mesh=mesh,
        in_specs=placed,
        out_specs=P(None, None, depth_axis, row_axis, None),
        check_vma=False,
    )
```

profile of v0, /device:TPU:1, one launch (start us, length us, event | category | flops | bytes accessed | tf_op | source)
XLA Modules:
  0.0 46.1 jit_solution(10224933861165372220)
XLA Ops:
  0.0 44.8 %shard_map.64 = f32[2,4,8,128]{3,2,1,0:T(8,128)} custom-call(s32[16,64]{1,0:T(8,128)} %live_ref.1, f32[2]{0:T(128)} %slopes_ref.1, f32[3]{0:T(128)} %palette_ref.1, s32[2,16]{1,0:T(2,128)} %order_ref.1, s32[2,16]{1,0:T(2,128)} %owner_ref.1, f32[8,128,128]{2,1,0:T(8,128)} %dens_ref.1), custom_call_target="tpu_custom_call" | custom-call | tf_op jit(solution)/shard_map/pallas_call | solution.py:324
  44.8 1.4 %copy.9 = f32[2,4,1,8,128]{4,3,2,1,0:T(8,128)} copy(f32[2,4,1,8,128]{4,3,2,1,0:T(8,128)} %bitcast.3) | data formatting | bytes 65536
where the time goes:
time: 46.4 us; the launch traced here: 46.1 us
  Pallas kernels  44.8 us (97%)
  local copies, waits for them, and re-layouts  1.38 us (3%)
    pallas_call x1, Pallas kernels, body(): pl.pallas_call(functools.partial(kernel, G, R, depth_axis, row_axis), out...  44.8 us
    unnamed x1, local copies, waits for them, and re-layouts  1.38 us

commit v1 on v0

--- a/solution.py
+++ b/solution.py
@@ -160,18 +160,15 @@
         lax.fori_loop(0, CZ + 2, layer, 0)
 
     def smooth_cols(lo, hi):
-        def layer(z, carry):
-            x = rowed[z, lo:hi, :]
-            high = x.astype(BF16)
-            low = (x - high.astype(F32)).astype(BF16)
-            both = jnp.dot(
-                jnp.concatenate([high, low], axis=1), band[...], preferred_element_type=F32
-            )
-            smooth[z, lo:hi, :] = both[:, 0:W]
-            dcol[z, lo:hi, :] = both[:, W : 2 * W]
-            return carry
-
-        lax.fori_loop(0, CZ + 2, layer, 0)
+        n = (CZ + 2) * (hi - lo)
+        x = rowed[:, lo:hi, :].reshape(n, W)
+        high = x.astype(BF16)
+        low = (x - high.astype(F32)).astype(BF16)
+        both = jnp.dot(
+            jnp.concatenate([high, low], axis=1), band[...], preferred_element_type=F32
+        )
+        smooth[:, lo:hi, :] = both[:, 0:W].reshape(CZ + 2, hi - lo, W)
+        dcol[:, lo:hi, :] = both[:, W : 2 * W].reshape(CZ + 2, hi - lo, W)
 
     def shade(lo, hi):
         def layer(z, carry):
@@ -196,13 +193,10 @@
         lax.fori_loop(0, CZ, layer, 0)
 
     def shear_rows(lo, hi):
-        def layer(z, carry):
+        for z in range(CZ):
             lhs = layers[z, :, lo:hi, :].reshape(2 * (hi - lo), W)
             out = jnp.dot(lhs, shear[z], preferred_element_type=F32)
             sheared[z, :, lo // TR : hi // TR] = out.reshape(2, (hi - lo) // TR, TR, 2 * W)
-            return carry
-
-        lax.fori_loop(0, CZ, layer, 0)
 
     def clear(lo, hi):
         for dz in (-1, 1):

time: 46.4 us -> 38.1 us (0.82)
  Pallas kernels: 44.8 us -> 36.4 us
    pallas_call x1, Pallas kernels: 44.8 us -> 36.4 us  [body(): pl.pallas_call(functools.partial(kernel, G, R, depth_axis, row_axis), out...]
where the time goes in v1:
time: 38.1 us; the launch traced here: 37.8 us
  Pallas kernels  36.4 us (96%)
  local copies, waits for them, and re-layouts  1.38 us (4%)
    pallas_call x1, Pallas kernels, body(): pl.pallas_call(functools.partial(kernel, G, R, depth_axis, row_axis), out...  36.4 us
    unnamed x1, local copies, waits for them, and re-layouts  1.38 us

profile of v1, /device:TPU:1, one launch (start us, length us, event | category | flops | bytes accessed | tf_op | source)
XLA Modules:
  0.0 37.8 jit_solution(3210877296005609938)
XLA Ops:
  0.0 36.4 %shard_map.64 = f32[2,4,8,128]{3,2,1,0:T(8,128)} custom-call(s32[16,64]{1,0:T(8,128)} %live_ref.1, f32[2]{0:T(128)} %slopes_ref.1, f32[3]{0:T(128)} %palette_ref.1, s32[2,16]{1,0:T(2,128)} %order_ref.1, s32[2,16]{1,0:T(2,128)} %owner_ref.1, f32[8,128,128]{2,1,0:T(8,128)} %dens_ref.1), custom_call_target="tpu_custom_call" | custom-call | tf_op jit(solution)/shard_map/pallas_call | solution.py:318
  36.5 1.4 %copy.9 = f32[2,4,1,8,128]{4,3,2,1,0:T(8,128)} copy(f32[2,4,1,8,128]{4,3,2,1,0:T(8,128)} %bitcast.3) | data formatting | bytes 65536

commit v2 on v1

--- a/solution.py
+++ b/solution.py
@@ -22,7 +22,7 @@
     live_ref, slopes_ref, palette_ref, order_ref, owner_ref, dens_ref,
     out_ref,
     ext, summed, rowed, smooth, dcol, band, layers, shear, sheared, outbox, inbox, inverse,
-    local_sem, zsend, zrecv, rsend, rrecv, tsend, trecv,
+    local_sem, zsend, zrecv, rsend, rrecv, tsend, trecv, known,
 ):
     me = lax.axis_index(depth_axis)
     col = lax.axis_index(row_axis)
@@ -35,11 +35,11 @@
 
     barrier = pltpu.get_barrier_semaphore()
 
-    def greet(k, carry):
-        pl.semaphore_signal(barrier, inc=1, device_id=at(lax.rem(me + k, G), col))
-        return carry
-
-    lax.fori_loop(1, G, greet, 0)
+    def ring(k):
+        return at(lax.rem(me + (k + G), G), col)
+
+    for k in (-1, 1):
+        pl.semaphore_signal(barrier, inc=1, device_id=ring(k))
     for dr in (-1, 1):
         for dz in (-1, 0, 1):
             ok = hasr[dr] if dz == 0 else hasr[dr] & has[dz]
@@ -52,7 +52,17 @@
     local.start()
     beside = hasr[-1].astype(jnp.int32) + hasr[1].astype(jnp.int32)
     above = has[-1].astype(jnp.int32) + has[1].astype(jnp.int32)
-    pl.semaphore_wait(barrier, (G - 1) + beside * (1 + above))
+    pl.semaphore_wait(barrier, 2 + beside * (1 + above))
+
+    rounds = [1 << j for j in range((G // 4).bit_length())]
+
+    def tell(j):
+        for side, sign in enumerate((1, -1)):
+            pl.semaphore_signal(known.at[j, side], inc=1, device_id=ring(sign * rounds[j]))
+
+    def hear(j):
+        for side in range(2):
+            pl.semaphore_wait(known.at[j, side], 1)
 
     def zcopy(dz, k):
         lo, hi = CHUNKS[k]
@@ -91,6 +101,8 @@
         def _():
             for k in range(1, NC):
                 zcopy(dz, k).start()
+
+    tell(0)
 
     for dz in (1, -1):
         @pl.when(jnp.logical_not(has[-dz]))
@@ -204,6 +216,9 @@
             def _():
                 smooth[0 if dz == -1 else CZ + 1, lo:hi, :] = jnp.zeros((hi - lo, W), F32)
 
+    hear(0)
+    if len(rounds) > 1:
+        tell(1)
     local.wait()
     for dz, dr in rcopies:
         @pl.when(allowed(-dz, -dr))
@@ -238,11 +253,21 @@
         shade(done_rows, shaded)
         shear_rows(done_rows, shaded)
         done_rows = shaded
+        if k + 1 < len(rounds):
+            hear(k + 1)
+            if k + 2 < len(rounds):
+                tell(k + 2)
 
     def tcopy(d):
         return pltpu.make_async_remote_copy(
             outbox.at[d], inbox.at[me], tsend.at[d], trecv.at[me], device_id=at(d, col)
         )
+
+    def coded(x):
+        return (jnp.sqrt(jnp.minimum(x, 1.0)) * 65535.0 + 0.5).astype(jnp.int32)
+
+    full = 1.0625 * brightest
+    per_full = 1.0 / full
 
     def march(d, box, slot):
         for v in range(2):
@@ -253,16 +278,24 @@
                 a = sheared[z, 1, tile, :, v * W : v * W + W]
                 shaded = b if shaded is None else shaded + transmit * b
                 transmit = 1.0 - a if transmit is None else transmit * (1.0 - a)
-            box[slot, v, 0] = shaded
-            box[slot, v, 1] = transmit
-
-    def send(k, carry):
-        d = lax.rem(me + k, G)
+            box[slot, v] = (coded(shaded * per_full) << 16) | coded(1.0 - transmit)
+
+    def peer(i):
+        j = i // 2
+        chip = lax.rem(me // 2 + G // 4 + (j + 1) // 2 * (1 - 2 * lax.rem(j, 2)) + G // 2, G // 2)
+        return 2 * chip + lax.rem(i + me, 2)
+
+    other = me + 1 - 2 * lax.rem(me, 2)
+
+    def send(i, carry):
+        d = peer(i)
         march(d, outbox, d)
         tcopy(d).start()
         return carry
 
-    lax.fori_loop(1, G, send, 0)
+    lax.fori_loop(0, G - 2, send, 0)
+    march(other, outbox, other)
+    tcopy(other).start()
     march(me, inbox, me)
 
     def receive(k, carry):
@@ -278,13 +311,16 @@
         def blend(i, carry):
             shaded, transmit = carry
             s = order_ref[v, i]
-            return shaded + transmit * inbox[s, v, 0], transmit * inbox[s, v, 1]
+            word = inbox[s, v]
+            c = ((word >> 16) & 65535).astype(F32) * (1.0 / 65535.0)
+            a = (word & 65535).astype(F32) * (1.0 / 65535.0)
+            return shaded + transmit * (c * c), transmit * (1.0 - a * a)
 
         shaded, transmit = lax.fori_loop(
             0, G, blend, (jnp.zeros((TR, W), F32), jnp.ones((TR, W), F32)), unroll=True
         )
         for c in range(3):
-            out_ref[v, c] = shaded * (palette_ref[c] / brightest)
+            out_ref[v, c] = shaded * (palette_ref[c] * 1.0625)
         out_ref[v, 3] = 1.0 - transmit
 
     for dz in (1, -1):
@@ -330,8 +366,8 @@
                 pltpu.VMEM((CZ, 2, CY, W), BF16),
                 pltpu.VMEM((CZ, W, 2 * W), BF16),
                 pltpu.VMEM((CZ, 2, G, TR, 2 * W), F32),
-                pltpu.VMEM((G, 2, 2, TR, W), F32),
-                pltpu.VMEM((G, 2, 2, TR, W), F32),
+                pltpu.VMEM((G, 2, TR, W), jnp.int32),
+                pltpu.VMEM((G, 2, TR, W), jnp.int32),
                 pltpu.SMEM((2, G), jnp.int32),
                 dma,
                 dma((2, NC)),
@@ -340,6 +376,7 @@
                 dma((2, 3)),
                 dma((G,)),
                 dma((G,)),
+                pltpu.SemaphoreType.REGULAR((3, 2)),
             ],
             compiler_params=pltpu.CompilerParams(collective_id=0, has_side_effects=True),
         )(live_slices, shear_slopes, palette, depth_order, tile_owner, density)

time: 38.1 us -> 32.6 us (0.86)
  Pallas kernels: 36.4 us -> 31 us
    pallas_call x1, Pallas kernels: 36.4 us -> 31 us  [body(): pl.pallas_call(functools.partial(kernel, G, R, depth_axis, row_axis), out...]
where the time goes in v2:
time: 32.6 us; the launch traced here: 32.4 us
  Pallas kernels  31 us (95%)
  local copies, waits for them, and re-layouts  1.38 us (4%)
    pallas_call x1, Pallas kernels, body(): pl.pallas_call(functools.partial(kernel, G, R, depth_axis, row_axis), out...  31 us
    unnamed x1, local copies, waits for them, and re-layouts  1.38 us

profile of v2, /device:TPU:1, one launch (start us, length us, event | category | flops | bytes accessed | tf_op | source)
XLA Modules:
  0.0 32.4 jit_solution(2055588966967577517)
XLA Ops:
  0.0 31.0 %shard_map.64 = f32[2,4,8,128]{3,2,1,0:T(8,128)} custom-call(s32[16,64]{1,0:T(8,128)} %live_ref.1, f32[2]{0:T(128)} %slopes_ref.1, f32[3]{0:T(128)} %palette_ref.1, s32[2,16]{1,0:T(2,128)} %order_ref.1, s32[2,16]{1,0:T(2,128)} %owner_ref.1, f32[8,128,128]{2,1,0:T(8,128)} %dens_ref.1), custom_call_target="tpu_custom_call" | custom-call | tf_op jit(solution)/shard_map/pallas_call | solution.py:354
  31.0 1.4 %copy.9 = f32[2,4,1,8,128]{4,3,2,1,0:T(8,128)} copy(f32[2,4,1,8,128]{4,3,2,1,0:T(8,128)} %bitcast.3) | data formatting | bytes 65536

commit v3 on v2

--- a/solution.py
+++ b/solution.py
@@ -147,6 +147,10 @@
     live = live_ref[me, col]
     brightest = jnp.maximum(jnp.maximum(palette_ref[0], palette_ref[1]), palette_ref[2])
 
+    ambient = 0.25 * brightest
+    light = [0.75 * part * brightest for part in LIGHT]
+    rate = -3.0 * LOG2E / (CZ * G)
+
     def depth_sums(lo, hi):
         def block(b, carry):
             rows = pl.ds(pl.multiple_of(lo + 8 * b, 8), 8)
@@ -158,7 +162,8 @@
                 summed[z, rows, :] = eight[z] + x[z + 8]
             return carry
 
-        lax.fori_loop(0, (hi - lo) // 8, block, 0)
+        n = (hi - lo) // 8
+        lax.fori_loop(0, n, block, 0, unroll=True)
 
     def smooth_rows(lo, hi):
         def layer(z, carry):
@@ -169,7 +174,7 @@
                 )
             return carry
 
-        lax.fori_loop(0, CZ + 2, layer, 0)
+        lax.fori_loop(0, CZ + 2, layer, 0, unroll=True)
 
     def smooth_cols(lo, hi):
         n = (CZ + 2) * (hi - lo)
@@ -184,8 +189,7 @@
 
     def shade(lo, hi):
         def layer(z, carry):
-            alive = (z < live).astype(jnp.int32).astype(F32)
-            bright_of = alive * brightest
+            fade = rate * (z < live).astype(jnp.int32).astype(F32)
             for r in range(lo, hi, 16):
                 q = r + 4
                 n = 16
@@ -193,16 +197,17 @@
                 dz = smooth[z + 2, q : q + n, :] - smooth[z, q : q + n, :]
                 dr = smooth[z + 1, q + 1 : q + n + 1, :] - smooth[z + 1, q - 1 : q + n - 1, :]
                 dc = dcol[z + 1, q : q + n, :]
-                along = jnp.maximum(0.0, LIGHT[0] * dz + LIGHT[1] * dr + LIGHT[2] * dc)
-                facing = along * lax.rsqrt(dz * dz + dr * dr + dc * dc + 0.01 * 1458.0 * 1458.0)
-                y = center * (2.0 / 729.0)
-                soft = jnp.maximum(y, 0.0) + jnp.log(1.0 + jnp.exp(-jnp.abs(y)))
-                opacity = 1.0 - jnp.exp(soft * (-3.0 / (CZ * G)))
-                layers[z, 0, r : r + n, :] = (opacity * (0.25 + 0.75 * facing) * bright_of).astype(BF16)
-                layers[z, 1, r : r + n, :] = (opacity * alive).astype(BF16)
+                along = jnp.maximum(0.0, light[0] * dz + light[1] * dr + light[2] * dc)
+                lit = ambient + along * lax.rsqrt((dz * dz + 0.01 * 1458.0 * 1458.0) + (dr * dr + dc * dc))
+                soft = jnp.maximum(center * (2.0 / 729.0), 0.0) + jnp.log(
+                    1.0 + jnp.exp2(jnp.abs(center) * (-2.0 * LOG2E / 729.0))
+                )
+                opacity = 1.0 - jnp.exp2(soft * fade)
+                layers[z, 0, r : r + n, :] = (opacity * lit).astype(BF16)
+                layers[z, 1, r : r + n, :] = opacity.astype(BF16)
             return carry
 
-        lax.fori_loop(0, CZ, layer, 0)
+        lax.fori_loop(0, CZ, layer, 0, unroll=True)
 
     def shear_rows(lo, hi):
         for z in range(CZ):
@@ -228,6 +233,7 @@
     depth_sums(0, 8)
     depth_sums(CY + 8, CY + 16)
     done_rows, done_smooth = 0, 0
+    pending = None
     for k in range(NC):
         for dz in (1, -1):
             @pl.when(has[-dz])
@@ -238,6 +244,8 @@
         last = k == NC - 1
         upto = CY + 8 if last else hi
         smooth_rows(done_smooth, upto)
+        if pending is not None:
+            shear_rows(*pending)
         smooth_cols(done_smooth, upto)
         clear(done_smooth, upto)
         if k == 0:
@@ -251,16 +259,18 @@
         done_smooth = upto
         shaded = CY if last else hi - 16
         shade(done_rows, shaded)
-        shear_rows(done_rows, shaded)
+        pending = (done_rows, shaded)
         done_rows = shaded
         if k + 1 < len(rounds):
             hear(k + 1)
             if k + 2 < len(rounds):
                 tell(k + 2)
 
+    shear_rows(*pending)
+
     def tcopy(d):
         return pltpu.make_async_remote_copy(
-            outbox.at[d], inbox.at[me], tsend.at[d], trecv.at[me], device_id=at(d, col)
+            outbox.at[d], inbox.at[me], tsend, trecv, device_id=at(d, col)
         )
 
     def coded(x):
@@ -293,19 +303,15 @@
         tcopy(d).start()
         return carry
 
-    lax.fori_loop(0, G - 2, send, 0)
+    lax.fori_loop(0, G - 2, send, 0, unroll=2)
     march(other, outbox, other)
     tcopy(other).start()
     march(me, inbox, me)
 
-    def receive(k, carry):
-        s = lax.rem(me + G - k, G)
-        pltpu.make_async_remote_copy(
-            outbox.at[s], inbox.at[s], tsend.at[s], trecv.at[s], device_id=at(s, col)
-        ).wait_recv()
-        return carry
-
-    lax.fori_loop(1, G, receive, 0)
+    others = pltpu.make_async_remote_copy(
+        outbox.at[0 : G - 1], inbox.at[0 : G - 1], tsend, trecv, device_id=at(other, col)
+    )
+    others.wait_recv()
 
     for v in range(2):
         def blend(i, carry):
@@ -333,12 +339,7 @@
         def _():
             rcopy(dz, dr).wait_send()
 
-    def sent(k, carry):
-        d = lax.rem(me + k, G)
-        tcopy(d).wait_send()
-        return carry
-
-    lax.fori_loop(1, G, sent, 0)
+    others.wait_send()
 
 
 def solution(mesh):
@@ -374,8 +375,8 @@
                 dma((2, NC)),
                 dma((2, 3)),
                 dma((2, 3)),
-                dma((G,)),
-                dma((G,)),
+                dma,
+                dma,
                 pltpu.SemaphoreType.REGULAR((3, 2)),
             ],
             compiler_params=pltpu.CompilerParams(collective_id=0, has_side_effects=True),

time: 32.6 us -> 30.6 us (0.939)
  Pallas kernels: 31 us -> 29 us
    pallas_call x1, Pallas kernels: 31 us -> 29 us  [body(): pl.pallas_call(functools.partial(kernel, G, R, depth_axis, row_axis), out...]
where the time goes in v3:
time: 30.6 us; the launch traced here: 30.4 us
  Pallas kernels  29 us (95%)
  local copies, waits for them, and re-layouts  1.38 us (5%)
    pallas_call x1, Pallas kernels, body(): pl.pallas_call(functools.partial(kernel, G, R, depth_axis, row_axis), out...  29 us
    unnamed x1, local copies, waits for them, and re-layouts  1.38 us

profile of v3, /device:TPU:1, one launch (start us, length us, event | category | flops | bytes accessed | tf_op | source)
XLA Modules:
  0.0 30.4 jit_solution(4719642617198842030)
XLA Ops:
  0.0 29.0 %shard_map.64 = f32[2,4,8,128]{3,2,1,0:T(8,128)} custom-call(s32[16,64]{1,0:T(8,128)} %live_ref.1, f32[2]{0:T(128)} %slopes_ref.1, f32[3]{0:T(128)} %palette_ref.1, s32[2,16]{1,0:T(2,128)} %order_ref.1, s32[2,16]{1,0:T(2,128)} %owner_ref.1, f32[8,128,128]{2,1,0:T(8,128)} %dens_ref.1), custom_call_target="tpu_custom_call" | custom-call | tf_op jit(solution)/shard_map/pallas_call | solution.py:355
  29.0 1.4 %copy.9 = f32[2,4,1,8,128]{4,3,2,1,0:T(8,128)} copy(f32[2,4,1,8,128]{4,3,2,1,0:T(8,128)} %bitcast.3) | data formatting | bytes 65536

commit v4 on v3

--- a/solution.py
+++ b/solution.py
@@ -9,7 +9,13 @@
 
 LIGHT = (0.48, 0.6, 0.64)
 LOG2E = 1.4426950408889634
-CHUNKS = ((0, 32), (32, 64), (64, 96), (96, 128))
+CHUNKS = ((0, 48), (48, 80), (80, 112), (112, 128))
+WORK = (
+    {"rows": ((8, 48),), "shade": ((16, 32),)},
+    {"rows": ((48, 80),), "shade": ((32, 64),)},
+    {"rows": ((80, 112), (0, 8)), "shade": ((64, 96), (0, 16))},
+    {"rows": ((112, 136),), "shade": ((96, 128),)},
+)
 F32, BF16 = jnp.float32, jnp.bfloat16
 
 
@@ -19,10 +25,10 @@
 
 def kernel(
     G, R, depth_axis, row_axis,
-    live_ref, slopes_ref, palette_ref, order_ref, owner_ref, dens_ref,
+    live_hbm, slopes_hbm, palette_hbm, order_hbm, owner_hbm, dens_ref,
     out_ref,
     ext, summed, rowed, smooth, dcol, band, layers, shear, sheared, outbox, inbox, inverse,
-    local_sem, zsend, zrecv, rsend, rrecv, tsend, trecv, known,
+    live_ref, slopes_ref, palette_ref, order_ref, owner_ref, table_sem, local_sem, zsend, zrecv, rsend, rrecv, tsend, trecv, known,
 ):
     me = lax.axis_index(depth_axis)
     col = lax.axis_index(row_axis)
@@ -48,6 +54,17 @@
             def _():
                 pl.semaphore_signal(barrier, inc=1, device_id=at(me + dz, col + dr))
 
+    tables = [
+        pltpu.make_async_copy(a, b, table_sem.at[i])
+        for i, (a, b) in enumerate(
+            (
+                (owner_hbm, owner_ref), (slopes_hbm, slopes_ref), (live_hbm, live_ref),
+                (palette_hbm, palette_ref), (order_hbm, order_ref),
+            )
+        )
+    ]
+    for table in tables:
+        table.start()
     local = pltpu.make_async_copy(dens_ref, ext.at[5:13, 8:136, :], local_sem)
     local.start()
     beside = hasr[-1].astype(jnp.int32) + hasr[1].astype(jnp.int32)
@@ -114,6 +131,9 @@
         def _():
             rd = slice(0, 8) if dr == 1 else slice(136, 144)
             ext[:, rd, :] = jnp.zeros((CZ + 10, 8, W), F32)
+
+    for table in tables:
+        table.wait()
 
     def invert(d, carry):
         for v in range(2):
@@ -225,48 +245,50 @@
     if len(rounds) > 1:
         tell(1)
     local.wait()
-    for dz, dr in rcopies:
-        @pl.when(allowed(-dz, -dr))
-        def _():
-            rcopy(dz, dr).wait_recv()
-
-    depth_sums(0, 8)
-    depth_sums(CY + 8, CY + 16)
-    done_rows, done_smooth = 0, 0
-    pending = None
-    for k in range(NC):
+    def sides_in(dr):
+        for dz in (1, -1, 0):
+            @pl.when(allowed(-dz, -dr))
+            def _():
+                rcopy(dz, dr).wait_recv()
+
+    pending = []
+    for k, ((lo, hi), ranges) in enumerate(zip(CHUNKS, WORK)):
         for dz in (1, -1):
             @pl.when(has[-dz])
             def _():
                 zcopy(dz, k).wait_recv()
-        lo, hi = CHUNKS[k]
         depth_sums(8 + lo, 8 + hi)
-        last = k == NC - 1
-        upto = CY + 8 if last else hi
-        smooth_rows(done_smooth, upto)
-        if pending is not None:
-            shear_rows(*pending)
-        smooth_cols(done_smooth, upto)
-        clear(done_smooth, upto)
-        if k == 0:
-            @pl.when(jnp.logical_not(hasr[-1]))
-            def _():
-                smooth[:, 0:4, :] = jnp.zeros((CZ + 2, 4, W), F32)
-        if last:
-            @pl.when(jnp.logical_not(hasr[1]))
-            def _():
-                smooth[:, CY + 4 : CY + 8, :] = jnp.zeros((CZ + 2, 4, W), F32)
-        done_smooth = upto
-        shaded = CY if last else hi - 16
-        shade(done_rows, shaded)
-        pending = (done_rows, shaded)
-        done_rows = shaded
+        if ranges["rows"][-1][0] == 0:
+            sides_in(1)
+            depth_sums(0, 8)
+        if ranges["rows"][-1][1] == CY + 8:
+            sides_in(-1)
+            depth_sums(CY + 8, CY + 16)
+        for first, end in ranges["rows"]:
+            smooth_rows(first, end)
+        for job in pending:
+            shear_rows(*job)
+        for first, end in ranges["rows"]:
+            smooth_cols(first, end)
+            clear(first, end)
+            if first == 0:
+                @pl.when(jnp.logical_not(hasr[-1]))
+                def _():
+                    smooth[:, 0:4, :] = jnp.zeros((CZ + 2, 4, W), F32)
+            if end == CY + 8:
+                @pl.when(jnp.logical_not(hasr[1]))
+                def _():
+                    smooth[:, CY + 4 : CY + 8, :] = jnp.zeros((CZ + 2, 4, W), F32)
+        for job in ranges["shade"]:
+            shade(*job)
+        pending = ranges["shade"]
         if k + 1 < len(rounds):
             hear(k + 1)
             if k + 2 < len(rounds):
                 tell(k + 2)
 
-    shear_rows(*pending)
+    for job in pending:
+        shear_rows(*job)
 
     def tcopy(d):
         return pltpu.make_async_remote_copy(
@@ -290,20 +312,13 @@
                 transmit = 1.0 - a if transmit is None else transmit * (1.0 - a)
             box[slot, v] = (coded(shaded * per_full) << 16) | coded(1.0 - transmit)
 
-    def peer(i):
+    other = me + 1 - 2 * (me & 1)
+    for i in range(G - 2):
         j = i // 2
-        chip = lax.rem(me // 2 + G // 4 + (j + 1) // 2 * (1 - 2 * lax.rem(j, 2)) + G // 2, G // 2)
-        return 2 * chip + lax.rem(i + me, 2)
-
-    other = me + 1 - 2 * lax.rem(me, 2)
-
-    def send(i, carry):
-        d = peer(i)
+        away = G // 4 + (j + 1) // 2 * (1 - 2 * (j % 2))
+        d = 2 * ((me // 2 + away) & (G // 2 - 1)) + ((i + me) & 1)
         march(d, outbox, d)
         tcopy(d).start()
-        return carry
-
-    lax.fori_loop(0, G - 2, send, 0, unroll=2)
     march(other, outbox, other)
     tcopy(other).start()
     march(me, inbox, me)
@@ -311,6 +326,16 @@
     others = pltpu.make_async_remote_copy(
         outbox.at[0 : G - 1], inbox.at[0 : G - 1], tsend, trecv, device_id=at(other, col)
     )
+    for dz in (1, -1):
+        @pl.when(has[dz])
+        def _():
+            for k in range(NC):
+                zcopy(dz, k).wait_send()
+    for dz, dr in rcopies:
+        @pl.when(allowed(dz, dr))
+        def _():
+            rcopy(dz, dr).wait_send()
+    others.wait_send()
     others.wait_recv()
 
     for v in range(2):
@@ -329,18 +354,6 @@
             out_ref[v, c] = shaded * (palette_ref[c] * 1.0625)
         out_ref[v, 3] = 1.0 - transmit
 
-    for dz in (1, -1):
-        @pl.when(has[dz])
-        def _():
-            for k in range(NC):
-                zcopy(dz, k).wait_send()
-    for dz, dr in rcopies:
-        @pl.when(allowed(dz, dr))
-        def _():
-            rcopy(dz, dr).wait_send()
-
-    others.wait_send()
-
 
 def solution(mesh):
     depth_axis, row_axis = mesh.axis_names
@@ -349,13 +362,13 @@
     def body(density, live_slices, shear_slopes, palette, depth_order, tile_owner):
         CZ, CY, W = density.shape
         TR = CY // G
-        smem = pl.BlockSpec(memory_space=pltpu.SMEM)
+        arrays = (live_slices, shear_slopes, palette, depth_order, tile_owner, density)
         dma = pltpu.SemaphoreType.DMA
         NC = len(CHUNKS)
         out = pl.pallas_call(
             functools.partial(kernel, G, R, depth_axis, row_axis),
             out_shape=jax.ShapeDtypeStruct((2, 4, TR, W), F32),
-            in_specs=[smem] * 5 + [pl.BlockSpec(memory_space=pl.ANY)],
+            in_specs=[pl.BlockSpec(memory_space=pl.ANY)] * 6,
             out_specs=pl.BlockSpec(memory_space=pltpu.VMEM),
             scratch_shapes=[
                 pltpu.VMEM((CZ + 10, CY + 16, W), F32),
@@ -370,6 +383,8 @@
                 pltpu.VMEM((G, 2, TR, W), jnp.int32),
                 pltpu.VMEM((G, 2, TR, W), jnp.int32),
                 pltpu.SMEM((2, G), jnp.int32),
+                *(pltpu.SMEM(a.shape, a.dtype) for a in arrays[:5]),
+                dma((5,)),
                 dma,
                 dma((2, NC)),
                 dma((2, NC)),
@@ -379,8 +394,8 @@
                 dma,
                 pltpu.SemaphoreType.REGULAR((3, 2)),
             ],
-            compiler_params=pltpu.CompilerParams(collective_id=0, has_side_effects=True),
-        )(live_slices, shear_slopes, palette, depth_order, tile_owner, density)
+            compiler_params=pltpu.CompilerParams(collective_id=0, has_side_effects=True, vmem_limit_bytes=12 << 20),
+        )(*(pltpu.with_memory_space_constraint(a, pltpu.HBM) for a in arrays))
         return out[:, :, None]
 
     placed = (P(depth_axis, row_axis, None), P(), P(), P(), P(), P())

time: 30.6 us -> 28.1 us (0.918)
  Pallas kernels: 29 us -> 27.3 us
  local copies, waits for them, and re-layouts: 1.38 us -> 0.62 us
    pallas_call x1, Pallas kernels: 29 us -> 27.3 us  [body(): pl.pallas_call(functools.partial(kernel, G, R, depth_axis, row_axis), out...]
    unnamed x1, local copies, waits for them, and re-layouts: 1.38 us -> 0.62 us
where the time goes in v4:
time: 28.1 us; the launch traced here: 28 us
  Pallas kernels  27.3 us (97%)
  local copies, waits for them, and re-layouts  0.62 us (2%)
    pallas_call x1, Pallas kernels, body(): pl.pallas_call(functools.partial(kernel, G, R, depth_axis, row_axis), out...  27.3 us
    unnamed x1, local copies, waits for them, and re-layouts  0.62 us

profile of v4, /device:TPU:1, one launch (start us, length us, event | category | flops | bytes accessed | tf_op | source)
XLA Modules:
  0.0 28.0 jit_solution(2321303005451762034)
XLA Ops:
  0.0 27.3 %shard_map.64 = f32[2,4,8,128]{3,2,1,0:T(8,128)S(1)} custom-call(s32[16,64]{1,0:T(8,128)} %live_hbm.1, f32[2]{0:T(128)} %slopes_hbm.1, f32[3]{0:T(128)} %palette_hbm.1, s32[2,16]{1,0:T(2,128)} %order_hbm.1, s32[2,16]{1,0:T(2,128)} %owner_hbm.1, f32[8,128,128]{2,1,0:T(8,128)} %dens_ref.1), custom_call_target="tpu_custom_call" | custom-call | tf_op jit(solution)/shard_map/pallas_call | solution.py:368
  27.4 0.6 %copy.9 = f32[2,4,1,8,128]{4,3,2,1,0:T(8,128)} copy(f32[2,4,1,8,128]{4,3,2,1,0:T(8,128)S(1)} %bitcast.3) | data formatting | bytes 65536

commit v5 on v4

--- a/solution.py
+++ b/solution.py
@@ -9,12 +9,12 @@
 
 LIGHT = (0.48, 0.6, 0.64)
 LOG2E = 1.4426950408889634
-CHUNKS = ((0, 48), (48, 80), (80, 112), (112, 128))
+STEPS = 32767.0 / 96.0
+CHUNKS = ((0, 32), (32, 80), (80, 128))
 WORK = (
-    {"rows": ((8, 48),), "shade": ((16, 32),)},
-    {"rows": ((48, 80),), "shade": ((32, 64),)},
-    {"rows": ((80, 112), (0, 8)), "shade": ((64, 96), (0, 16))},
-    {"rows": ((112, 136),), "shade": ((96, 128),)},
+    {"rows": ((8, 32),), "shade": ()},
+    {"rows": ((32, 80), (0, 8)), "shade": ((16, 64), (0, 16))},
+    {"rows": ((80, 136),), "shade": ((64, 128),)},
 )
 F32, BF16 = jnp.float32, jnp.bfloat16
 
@@ -27,7 +27,7 @@
     G, R, depth_axis, row_axis,
     live_hbm, slopes_hbm, palette_hbm, order_hbm, owner_hbm, dens_ref,
     out_ref,
-    ext, summed, rowed, smooth, dcol, band, layers, shear, sheared, outbox, inbox, inverse,
+    raw, quant, codes, halo, side_rows, summed, rowed, smooth, dcol, band, layers, shear, sheared, outbox, inbox, inverse,
     live_ref, slopes_ref, palette_ref, order_ref, owner_ref, table_sem, local_sem, zsend, zrecv, rsend, rrecv, tsend, trecv, known,
 ):
     me = lax.axis_index(depth_axis)
@@ -65,8 +65,24 @@
     ]
     for table in tables:
         table.start()
-    local = pltpu.make_async_copy(dens_ref, ext.at[5:13, 8:136, :], local_sem)
-    local.start()
+    local = [
+        pltpu.make_async_copy(dens_ref.at[:, lo:hi, :], raw.at[:, lo:hi, :], local_sem.at[k])
+        for k, (lo, hi) in enumerate(CHUNKS)
+    ]
+    for part in local:
+        part.start()
+
+    def encode(k):
+        lo, hi = CHUNKS[k]
+        half = (hi - lo) // 2
+        local[k].wait()
+        for z in range(CZ):
+            x = jnp.round(raw[z, lo:hi, :] * STEPS)
+            quant[z, lo:hi, :] = x
+            i = x.astype(jnp.int32)
+            codes[z, lo // 2 : hi // 2, :] = (i[:half] << 16) + (i[half:] + 32768)
+
+    encode(0)
     beside = hasr[-1].astype(jnp.int32) + hasr[1].astype(jnp.int32)
     above = has[-1].astype(jnp.int32) + has[1].astype(jnp.int32)
     pl.semaphore_wait(barrier, 2 + beside * (1 + above))
@@ -82,9 +98,9 @@
             pl.semaphore_wait(known.at[j, side], 1)
 
     def zcopy(dz, k):
-        lo, hi = CHUNKS[k]
-        src = dens_ref.at[3:8, lo:hi, :] if dz == 1 else dens_ref.at[0:5, lo:hi, :]
-        dst = ext.at[0:5, 8 + lo : 8 + hi, :] if dz == 1 else ext.at[13:18, 8 + lo : 8 + hi, :]
+        rows = slice(CHUNKS[k][0] // 2, CHUNKS[k][1] // 2)
+        src = codes.at[3:8, rows, :] if dz == 1 else codes.at[0:5, rows, :]
+        dst = halo.at[(1 - dz) // 2, :, rows, :]
         side = (dz + 1) // 2
         return pltpu.make_async_remote_copy(
             src, dst, zsend.at[side, k], zrecv.at[side, k], device_id=at(me + dz, col)
@@ -92,10 +108,10 @@
 
     def rcopy(dz, dr):
         zs, zd = {0: (slice(0, 8), slice(5, 13)), 1: (slice(3, 8), slice(0, 5)), -1: (slice(0, 5), slice(13, 18))}[dz]
-        rs, rd = {1: (slice(120, 128), slice(0, 8)), -1: (slice(0, 8), slice(136, 144))}[dr]
+        rs, rd = {1: (slice(120, 128), 0), -1: (slice(0, 8), 1)}[dr]
         side = (dr + 1) // 2
         return pltpu.make_async_remote_copy(
-            dens_ref.at[zs, rs, :], ext.at[zd, rd, :], rsend.at[side, dz + 1], rrecv.at[side, dz + 1],
+            dens_ref.at[zs, rs, :], side_rows.at[rd, zd], rsend.at[side, dz + 1], rrecv.at[side, dz + 1],
             device_id=at(me + dz, col + dr),
         )
 
@@ -113,10 +129,11 @@
         @pl.when(allowed(dz, dr))
         def _():
             rcopy(dz, dr).start()
-    for dz in (1, -1):
-        @pl.when(has[dz])
-        def _():
-            for k in range(1, NC):
+    for k in range(1, NC):
+        encode(k)
+        for dz in (1, -1):
+            @pl.when(has[dz])
+            def _():
                 zcopy(dz, k).start()
 
     tell(0)
@@ -124,13 +141,13 @@
     for dz in (1, -1):
         @pl.when(jnp.logical_not(has[-dz]))
         def _():
+            halo[(1 - dz) // 2] = jnp.full((5, CY // 2, W), 32768, jnp.int32)
             zd = slice(0, 5) if dz == 1 else slice(13, 18)
-            ext[zd, :, :] = jnp.zeros((5, CY + 16, W), F32)
+            side_rows[:, zd] = jnp.zeros((2, 5, 8, W), F32)
     for dr in (1, -1):
         @pl.when(jnp.logical_not(hasr[-dr]))
         def _():
-            rd = slice(0, 8) if dr == 1 else slice(136, 144)
-            ext[:, rd, :] = jnp.zeros((CZ + 10, 8, W), F32)
+            side_rows[(1 - dr) // 2] = jnp.zeros((CZ + 10, 8, W), F32)
 
     for table in tables:
         table.wait()
@@ -171,19 +188,28 @@
     light = [0.75 * part * brightest for part in LIGHT]
     rate = -3.0 * LOG2E / (CZ * G)
 
-    def depth_sums(lo, hi):
-        def block(b, carry):
-            rows = pl.ds(pl.multiple_of(lo + 8 * b, 8), 8)
-            x = [ext[z, rows, :] for z in range(CZ + 10)]
-            two = [x[i] + x[i + 1] for i in range(CZ + 8)]
-            four = [two[i] + two[i + 2] for i in range(CZ + 6)]
-            eight = [four[i] + four[i + 4] for i in range(CZ + 2)]
-            for z in range(CZ + 2):
-                summed[z, rows, :] = eight[z] + x[z + 8]
-            return carry
-
-        n = (hi - lo) // 8
-        lax.fori_loop(0, n, block, 0, unroll=True)
+    def depth_sum(x, q):
+        two = [x[i] + x[i + 1] for i in range(CZ + 8)]
+        four = [two[i] + two[i + 2] for i in range(CZ + 6)]
+        eight = [four[i] + four[i + 4] for i in range(CZ + 2)]
+        for z in range(CZ + 2):
+            summed[z, q : q + 8, :] = eight[z] + x[z + 8]
+
+    def depth_sums(k):
+        lo, hi = CHUNKS[k]
+        half = (hi - lo) // 2
+        for b in range(0, half, 8):
+            words = [[halo[side, z, lo // 2 + b : lo // 2 + b + 8, :] for z in range(5)] for side in range(2)]
+            for part in range(2):
+                r = lo + part * half + b
+                below, above = [
+                    [((w >> 16) if part == 0 else (w & 65535) - 32768).astype(F32) for w in ws] for ws in words
+                ]
+                depth_sum(below + [quant[z, r : r + 8, :] for z in range(CZ)] + above, r + 8)
+
+    def side_sums(side):
+        x = [jnp.round(side_rows[side, z] * STEPS) for z in range(CZ + 10)]
+        depth_sum(x, side * (CY + 8))
 
     def smooth_rows(lo, hi):
         def layer(z, carry):
@@ -218,9 +244,9 @@
                 dr = smooth[z + 1, q + 1 : q + n + 1, :] - smooth[z + 1, q - 1 : q + n - 1, :]
                 dc = dcol[z + 1, q : q + n, :]
                 along = jnp.maximum(0.0, light[0] * dz + light[1] * dr + light[2] * dc)
-                lit = ambient + along * lax.rsqrt((dz * dz + 0.01 * 1458.0 * 1458.0) + (dr * dr + dc * dc))
-                soft = jnp.maximum(center * (2.0 / 729.0), 0.0) + jnp.log(
-                    1.0 + jnp.exp2(jnp.abs(center) * (-2.0 * LOG2E / 729.0))
+                lit = ambient + along * lax.rsqrt((dz * dz + 0.01 * (1458.0 * STEPS) ** 2) + (dr * dr + dc * dc))
+                soft = jnp.maximum(center * (2.0 / (729.0 * STEPS)), 0.0) + jnp.log(
+                    1.0 + jnp.exp2(jnp.abs(center) * (-2.0 * LOG2E / (729.0 * STEPS)))
                 )
                 opacity = 1.0 - jnp.exp2(soft * fade)
                 layers[z, 0, r : r + n, :] = (opacity * lit).astype(BF16)
@@ -244,7 +270,6 @@
     hear(0)
     if len(rounds) > 1:
         tell(1)
-    local.wait()
     def sides_in(dr):
         for dz in (1, -1, 0):
             @pl.when(allowed(-dz, -dr))
@@ -252,18 +277,18 @@
                 rcopy(dz, dr).wait_recv()
 
     pending = []
-    for k, ((lo, hi), ranges) in enumerate(zip(CHUNKS, WORK)):
+    for k, ranges in enumerate(WORK):
         for dz in (1, -1):
             @pl.when(has[-dz])
             def _():
                 zcopy(dz, k).wait_recv()
-        depth_sums(8 + lo, 8 + hi)
+        depth_sums(k)
         if ranges["rows"][-1][0] == 0:
             sides_in(1)
-            depth_sums(0, 8)
+            side_sums(0)
         if ranges["rows"][-1][1] == CY + 8:
             sides_in(-1)
-            depth_sums(CY + 8, CY + 16)
+            side_sums(1)
         for first, end in ranges["rows"]:
             smooth_rows(first, end)
         for job in pending:
@@ -313,12 +338,14 @@
             box[slot, v] = (coded(shaded * per_full) << 16) | coded(1.0 - transmit)
 
     other = me + 1 - 2 * (me & 1)
-    for i in range(G - 2):
-        j = i // 2
+    for j in range(G // 2 - 1):
         away = G // 4 + (j + 1) // 2 * (1 - 2 * (j % 2))
-        d = 2 * ((me // 2 + away) & (G // 2 - 1)) + ((i + me) & 1)
-        march(d, outbox, d)
-        tcopy(d).start()
+        chip = 2 * ((me // 2 + away) & (G // 2 - 1))
+        pair = (chip + (me & 1), chip + 1 - (me & 1))
+        for d in pair:
+            march(d, outbox, d)
+        for d in pair:
+            tcopy(d).start()
     march(other, outbox, other)
     tcopy(other).start()
     march(me, inbox, me)
@@ -371,7 +398,11 @@
             in_specs=[pl.BlockSpec(memory_space=pl.ANY)] * 6,
             out_specs=pl.BlockSpec(memory_space=pltpu.VMEM),
             scratch_shapes=[
-                pltpu.VMEM((CZ + 10, CY + 16, W), F32),
+                pltpu.VMEM((CZ, CY, W), F32),
+                pltpu.VMEM((CZ, CY, W), F32),
+                pltpu.VMEM((CZ, CY // 2, W), jnp.int32),
+                pltpu.VMEM((2, 5, CY // 2, W), jnp.int32),
+                pltpu.VMEM((2, CZ + 10, 8, W), F32),
                 pltpu.VMEM((CZ + 2, CY + 16, W), F32),
                 pltpu.VMEM((CZ + 2, CY + 8, W), F32),
                 pltpu.VMEM((CZ + 2, CY + 8, W), F32),
@@ -385,7 +416,7 @@
                 pltpu.SMEM((2, G), jnp.int32),
                 *(pltpu.SMEM(a.shape, a.dtype) for a in arrays[:5]),
                 dma((5,)),
-                dma,
+                dma((NC,)),
                 dma((2, NC)),
                 dma((2, NC)),
                 dma((2, 3)),

time: 28.1 us -> 27.5 us (0.979)
  Pallas kernels: 27.3 us -> 26.7 us
    pallas_call x1, Pallas kernels: 27.3 us -> 26.7 us  [body(): pl.pallas_call(functools.partial(kernel, G, R, depth_axis, row_axis), out...]
where the time goes in v5:
time: 27.5 us; the launch traced here: 27.3 us
  Pallas kernels  26.7 us (97%)
  local copies, waits for them, and re-layouts  0.62 us (2%)
    pallas_call x1, Pallas kernels, body(): pl.pallas_call(functools.partial(kernel, G, R, depth_axis, row_axis), out...  26.7 us
    unnamed x1, local copies, waits for them, and re-layouts  0.62 us

profile of v5, /device:TPU:1, one launch (start us, length us, event | category | flops | bytes accessed | tf_op | source)
XLA Modules:
  0.0 27.3 jit_solution(2722918555193249330)
XLA Ops:
  0.0 26.7 %shard_map.64 = f32[2,4,8,128]{3,2,1,0:T(8,128)S(1)} custom-call(s32[16,64]{1,0:T(8,128)} %live_hbm.1, f32[2]{0:T(128)} %slopes_hbm.1, f32[3]{0:T(128)} %palette_hbm.1, s32[2,16]{1,0:T(2,128)} %order_hbm.1, s32[2,16]{1,0:T(2,128)} %owner_hbm.1, f32[8,128,128]{2,1,0:T(8,128)} %dens_ref.1), custom_call_target="tpu_custom_call" | custom-call | tf_op jit(solution)/shard_map/pallas_call | solution.py:395
  26.7 0.6 %copy.9 = f32[2,4,1,8,128]{4,3,2,1,0:T(8,128)} copy(f32[2,4,1,8,128]{4,3,2,1,0:T(8,128)S(1)} %bitcast.3) | data formatting | bytes 65536

commit v6 on v5

--- a/solution.py
+++ b/solution.py
@@ -27,7 +27,7 @@
     G, R, depth_axis, row_axis,
     live_hbm, slopes_hbm, palette_hbm, order_hbm, owner_hbm, dens_ref,
     out_ref,
-    raw, quant, codes, halo, side_rows, summed, rowed, smooth, dcol, band, layers, shear, sheared, outbox, inbox, inverse,
+    raw, quant, codes, halo, side_rows, summed, rowed, smooth, dcol, band, layers, shear, sheared, outbox, inbox, inverse, power,
     live_ref, slopes_ref, palette_ref, order_ref, owner_ref, table_sem, local_sem, zsend, zrecv, rsend, rrecv, tsend, trecv, known,
 ):
     me = lax.axis_index(depth_axis)
@@ -82,6 +82,49 @@
             i = x.astype(jnp.int32)
             codes[z, lo // 2 : hi // 2, :] = (i[:half] << 16) + (i[half:] + 32768)
 
+    for dz in (1, -1):
+        @pl.when(jnp.logical_not(has[-dz]))
+        def _():
+            halo[(1 - dz) // 2] = jnp.full((5, CY // 2, W), 32768, jnp.int32)
+            zd = slice(0, 5) if dz == 1 else slice(13, 18)
+            side_rows[:, zd] = jnp.zeros((2, 5, 8, W), F32)
+    for dr in (1, -1):
+        @pl.when(jnp.logical_not(hasr[-dr]))
+        def _():
+            side_rows[(1 - dr) // 2] = jnp.zeros((CZ + 10, 8, W), F32)
+
+    source = lax.broadcasted_iota(jnp.int32, (W, W), 0)
+    target = lax.broadcasted_iota(jnp.int32, (W, W), 1)
+    ones = spread(source, target, True)
+    diff = spread(source, target + 1, target + 1 < W) - spread(source, target - 1, target >= 1)
+    for half in range(2):
+        band[half * W : half * W + W, 0:W] = ones.astype(BF16)
+        band[half * W : half * W + W, W : 2 * W] = diff.astype(BF16)
+
+    for table in tables:
+        table.wait()
+
+    offset = (source - target).astype(F32)
+
+    def shears(z, carry):
+        depth = (me * CZ + z).astype(F32) + (0.5 - 0.5 * CZ * G)
+        for v in range(2):
+            m = jnp.maximum(0.0, 1.0 - jnp.abs(offset + slopes_ref[v] * depth))
+            shear[z, :, v * W : v * W + W] = m.astype(BF16)
+        return carry
+
+    lax.fori_loop(0, CZ, shears, 0)
+
+    for d in range(G):
+        for word in range(2):
+            power[word, d] = jnp.int32(16 ** (d % 8) if d // 8 == word else 0)
+    for v in range(2):
+        for word in range(2):
+            packed = jnp.int32(0)
+            for t in range(1, G):
+                packed = packed + t * power[word, owner_ref[v, t]]
+            inverse[v, word] = packed
+
     encode(0)
     beside = hasr[-1].astype(jnp.int32) + hasr[1].astype(jnp.int32)
     above = has[-1].astype(jnp.int32) + has[1].astype(jnp.int32)
@@ -121,6 +164,7 @@
     def allowed(dz, dr):
         return hasr[dr] if dz == 0 else hasr[dr] & has[dz]
 
+    tell(0)
     for dz in (1, -1):
         @pl.when(has[dz])
         def _():
@@ -135,51 +179,6 @@
             @pl.when(has[dz])
             def _():
                 zcopy(dz, k).start()
-
-    tell(0)
-
-    for dz in (1, -1):
-        @pl.when(jnp.logical_not(has[-dz]))
-        def _():
-            halo[(1 - dz) // 2] = jnp.full((5, CY // 2, W), 32768, jnp.int32)
-            zd = slice(0, 5) if dz == 1 else slice(13, 18)
-            side_rows[:, zd] = jnp.zeros((2, 5, 8, W), F32)
-    for dr in (1, -1):
-        @pl.when(jnp.logical_not(hasr[-dr]))
-        def _():
-            side_rows[(1 - dr) // 2] = jnp.zeros((CZ + 10, 8, W), F32)
-
-    for table in tables:
-        table.wait()
-
-    def invert(d, carry):
-        for v in range(2):
-            found = jnp.int32(0)
-            for t in range(G):
-                found = jnp.maximum(found, t * (owner_ref[v, t] == d).astype(jnp.int32))
-            inverse[v, d] = found
-        return carry
-
-    lax.fori_loop(0, G, invert, 0)
-
-    source = lax.broadcasted_iota(jnp.int32, (W, W), 0)
-    target = lax.broadcasted_iota(jnp.int32, (W, W), 1)
-    ones = spread(source, target, True)
-    diff = spread(source, target + 1, target + 1 < W) - spread(source, target - 1, target >= 1)
-    for half in range(2):
-        band[half * W : half * W + W, 0:W] = ones.astype(BF16)
-        band[half * W : half * W + W, W : 2 * W] = diff.astype(BF16)
-
-    offset = (source - target).astype(F32)
-
-    def shears(z, carry):
-        depth = (me * CZ + z).astype(F32) + (0.5 - 0.5 * CZ * G)
-        for v in range(2):
-            m = jnp.maximum(0.0, 1.0 - jnp.abs(offset + slopes_ref[v] * depth))
-            shear[z, :, v * W : v * W + W] = m.astype(BF16)
-        return carry
-
-    lax.fori_loop(0, CZ, shears, 0)
 
     live = live_ref[me, col]
     brightest = jnp.maximum(jnp.maximum(palette_ref[0], palette_ref[1]), palette_ref[2])
@@ -328,7 +327,7 @@
 
     def march(d, box, slot):
         for v in range(2):
-            tile = inverse[v, d]
+            tile = (inverse[v, d // 8] >> (4 * (d & 7))) & 15
             shaded, transmit = None, None
             for z in range(CZ) if v == 0 else range(CZ - 1, -1, -1):
                 b = sheared[z, 0, tile, :, v * W : v * W + W]
@@ -413,6 +412,7 @@
                 pltpu.VMEM((CZ, 2, G, TR, 2 * W), F32),
                 pltpu.VMEM((G, 2, TR, W), jnp.int32),
                 pltpu.VMEM((G, 2, TR, W), jnp.int32),
+                pltpu.SMEM((2, 2), jnp.int32),
                 pltpu.SMEM((2, G), jnp.int32),
                 *(pltpu.SMEM(a.shape, a.dtype) for a in arrays[:5]),
                 dma((5,)),

time: 27.5 us -> 27.4 us (level)
  no operation moved by 1% of the time
where the time goes in v6:
time: 27.4 us; the launch traced here: 27.2 us
  Pallas kernels  26.6 us (97%)
  local copies, waits for them, and re-layouts  0.62 us (2%)
    pallas_call x1, Pallas kernels, body(): pl.pallas_call(functools.partial(kernel, G, R, depth_axis, row_axis), out...  26.6 us
    unnamed x1, local copies, waits for them, and re-layouts  0.62 us

profile of v6, /device:TPU:1, one launch (start us, length us, event | category | flops | bytes accessed | tf_op | source)
XLA Modules:
  0.0 27.2 jit_solution(6898488981653366914)
XLA Ops:
  0.0 26.6 %shard_map.64 = f32[2,4,8,128]{3,2,1,0:T(8,128)S(1)} custom-call(s32[16,64]{1,0:T(8,128)} %live_hbm.1, f32[2]{0:T(128)} %slopes_hbm.1, f32[3]{0:T(128)} %palette_hbm.1, s32[2,16]{1,0:T(2,128)} %order_hbm.1, s32[2,16]{1,0:T(2,128)} %owner_hbm.1, f32[8,128,128]{2,1,0:T(8,128)} %dens_ref.1), custom_call_target="tpu_custom_call" | custom-call | tf_op jit(solution)/shard_map/pallas_call | solution.py:394
  26.6 0.6 %copy.9 = f32[2,4,1,8,128]{4,3,2,1,0:T(8,128)} copy(f32[2,4,1,8,128]{4,3,2,1,0:T(8,128)S(1)} %bitcast.3) | data formatting | bytes 65536

commit v7 on v6

--- a/solution.py
+++ b/solution.py
@@ -101,6 +101,61 @@
         band[half * W : half * W + W, 0:W] = ones.astype(BF16)
         band[half * W : half * W + W, W : 2 * W] = diff.astype(BF16)
 
+    encode(0)
+    beside = hasr[-1].astype(jnp.int32) + hasr[1].astype(jnp.int32)
+    above = has[-1].astype(jnp.int32) + has[1].astype(jnp.int32)
+    pl.semaphore_wait(barrier, 2 + beside * (1 + above))
+
+    rounds = [1 << j for j in range((G // 4).bit_length())]
+
+    def tell(j):
+        for side, sign in enumerate((1, -1)):
+            pl.semaphore_signal(known.at[j, side], inc=1, device_id=ring(sign * rounds[j]))
+
+    def hear(j):
+        for side in range(2):
+            pl.semaphore_wait(known.at[j, side], 1)
+
+    def zcopy(dz, k):
+        rows = slice(CHUNKS[k][0] // 2, CHUNKS[k][1] // 2)
+        src = codes.at[3:8, rows, :] if dz == 1 else codes.at[0:5, rows, :]
+        dst = halo.at[(1 - dz) // 2, :, rows, :]
+        side = (dz + 1) // 2
+        return pltpu.make_async_remote_copy(
+            src, dst, zsend.at[side, k], zrecv.at[side, k], device_id=at(me + dz, col)
+        )
+
+    def rcopy(dz, dr):
+        zs, zd = {0: (slice(0, 8), slice(5, 13)), 1: (slice(3, 8), slice(0, 5)), -1: (slice(0, 5), slice(13, 18))}[dz]
+        rs, rd = {1: (slice(120, 128), 0), -1: (slice(0, 8), 1)}[dr]
+        side = (dr + 1) // 2
+        return pltpu.make_async_remote_copy(
+            dens_ref.at[zs, rs, :], side_rows.at[rd, zd], rsend.at[side, dz + 1], rrecv.at[side, dz + 1],
+            device_id=at(me + dz, col + dr),
+        )
+
+    zcopies = [(dz, k) for k in range(NC) for dz in (1, -1)]
+    rcopies = [(dz, dr) for dr in (-1, 1) for dz in (1, -1, 0)]
+
+    def allowed(dz, dr):
+        return hasr[dr] if dz == 0 else hasr[dr] & has[dz]
+
+    tell(0)
+    for dz in (1, -1):
+        @pl.when(has[dz])
+        def _():
+            zcopy(dz, 0).start()
+    for dz, dr in rcopies:
+        @pl.when(allowed(dz, dr))
+        def _():
+            rcopy(dz, dr).start()
+    for k in range(1, NC):
+        encode(k)
+        for dz in (1, -1):
+            @pl.when(has[dz])
+            def _():
+                zcopy(dz, k).start()
+
     for table in tables:
         table.wait()
 
@@ -124,61 +179,6 @@
             for t in range(1, G):
                 packed = packed + t * power[word, owner_ref[v, t]]
             inverse[v, word] = packed
-
-    encode(0)
-    beside = hasr[-1].astype(jnp.int32) + hasr[1].astype(jnp.int32)
-    above = has[-1].astype(jnp.int32) + has[1].astype(jnp.int32)
-    pl.semaphore_wait(barrier, 2 + beside * (1 + above))
-
-    rounds = [1 << j for j in range((G // 4).bit_length())]
-
-    def tell(j):
-        for side, sign in enumerate((1, -1)):
-            pl.semaphore_signal(known.at[j, side], inc=1, device_id=ring(sign * rounds[j]))
-
-    def hear(j):
-        for side in range(2):
-            pl.semaphore_wait(known.at[j, side], 1)
-
-    def zcopy(dz, k):
-        rows = slice(CHUNKS[k][0] // 2, CHUNKS[k][1] // 2)
-        src = codes.at[3:8, rows, :] if dz == 1 else codes.at[0:5, rows, :]
-        dst = halo.at[(1 - dz) // 2, :, rows, :]
-        side = (dz + 1) // 2
-        return pltpu.make_async_remote_copy(
-            src, dst, zsend.at[side, k], zrecv.at[side, k], device_id=at(me + dz, col)
-        )
-
-    def rcopy(dz, dr):
-        zs, zd = {0: (slice(0, 8), slice(5, 13)), 1: (slice(3, 8), slice(0, 5)), -1: (slice(0, 5), slice(13, 18))}[dz]
-        rs, rd = {1: (slice(120, 128), 0), -1: (slice(0, 8), 1)}[dr]
-        side = (dr + 1) // 2
-        return pltpu.make_async_remote_copy(
-            dens_ref.at[zs, rs, :], side_rows.at[rd, zd], rsend.at[side, dz + 1], rrecv.at[side, dz + 1],
-            device_id=at(me + dz, col + dr),
-        )
-
-    zcopies = [(dz, k) for k in range(NC) for dz in (1, -1)]
-    rcopies = [(dz, dr) for dr in (-1, 1) for dz in (1, -1, 0)]
-
-    def allowed(dz, dr):
-        return hasr[dr] if dz == 0 else hasr[dr] & has[dz]
-
-    tell(0)
-    for dz in (1, -1):
-        @pl.when(has[dz])
-        def _():
-            zcopy(dz, 0).start()
-    for dz, dr in rcopies:
-        @pl.when(allowed(dz, dr))
-        def _():
-            rcopy(dz, dr).start()
-    for k in range(1, NC):
-        encode(k)
-        for dz in (1, -1):
-            @pl.when(has[dz])
-            def _():
-                zcopy(dz, k).start()
 
     live = live_ref[me, col]
     brightest = jnp.maximum(jnp.maximum(palette_ref[0], palette_ref[1]), palette_ref[2])

time: 27.4 us -> 27.6 us (level)
  no operation moved by 1% of the time
where the time goes in v7:
time: 27.6 us; the launch traced here: 27.4 us
  Pallas kernels  26.8 us (97%)
  local copies, waits for them, and re-layouts  0.62 us (2%)
    pallas_call x1, Pallas kernels, body(): pl.pallas_call(functools.partial(kernel, G, R, depth_axis, row_axis), out...  26.8 us
    unnamed x1, local copies, waits for them, and re-layouts  0.62 us

profile of v7, /device:TPU:1, one launch (start us, length us, event | category | flops | bytes accessed | tf_op | source)
XLA Modules:
  0.0 27.4 jit_solution(4345761510720576056)
XLA Ops:
  0.0 26.8 %shard_map.64 = f32[2,4,8,128]{3,2,1,0:T(8,128)S(1)} custom-call(s32[16,64]{1,0:T(8,128)} %live_hbm.1, f32[2]{0:T(128)} %slopes_hbm.1, f32[3]{0:T(128)} %palette_hbm.1, s32[2,16]{1,0:T(2,128)} %order_hbm.1, s32[2,16]{1,0:T(2,128)} %owner_hbm.1, f32[8,128,128]{2,1,0:T(8,128)} %dens_ref.1), custom_call_target="tpu_custom_call" | custom-call | tf_op jit(solution)/shard_map/pallas_call | solution.py:394
  26.8 0.6 %copy.9 = f32[2,4,1,8,128]{4,3,2,1,0:T(8,128)} copy(f32[2,4,1,8,128]{4,3,2,1,0:T(8,128)S(1)} %bitcast.3) | data formatting | bytes 65536
